TPU v7x, 256 devices: a whole 4x4x8 slice. The times are simulated.
256 devices in a mesh: ka: 4 (over z_hi, core), fit: 64 (over x, y, z_lo).
Axes of the slice: x: 4, y: 4, z: 8 (z_hi: 2, z_lo: 4; z = z_hi * 4 + z_lo), core: 2. Of those that a mesh axis runs over, the one named last changes fastest.
Arguments:
- integrals: bfloat16 [3, 4, 64, 48, 64, 128], P(None, 'ka', 'fit'), may hold values from -0.3125 to 0.3125
- block_lists: int32 [3, 4, 64, 2, 48], P(None, 'ka', 'fit'), may hold values from 0 to 15, as said below
- coeff: bfloat16 [4, 2, 1024, 256], P('ka', None, 'fit'), may hold values from -6 to 6
- match: int32 [3, 4], replicated, may hold values from 0 to 3, each once within a row
- ex_blocks: int32 [4, 2, 64], P('ka'), may hold values from 0 to 15, as said below
Outputs:
- exchange: float32 [4, 4096, 128], P('ka', 'fit')
Inputs may be any that keep to these rules, and one draw needn't show every extreme that they name: `block_lists`: each integral matrix lists 48 distinct blocks; each entry is a block index below 16, row first then column. `ex_blocks`: each k-point lists 64 distinct blocks, none on the diagonal (row block differs from column block).
All inputs are finite; a program needn't handle non-finite values.
Results may differ from a plain program's by a relative error of at most 0.0036.
Values may be sent and summed in bfloat16 or wider, within the bound.
A program may use at most 128 MiB of HBM per device.

v0:
```python
import jax
import jax.numpy as jnp
from jax import lax
from jax.sharding import PartitionSpec as P


def block_operands(coeff_one, edge):
    nblocks = coeff_one.shape[1] // edge
    real = coeff_one[0].reshape(nblocks, edge, -1)
    imag = coeff_one[1].reshape(nblocks, edge, -1)
    upper = jnp.concatenate([real, imag], axis=2)
    lower = jnp.concatenate([-imag, real], axis=2)
    return jnp.concatenate([upper, lower], axis=1)


def half_transform(lmat, lists, operands):
    nblocks = operands.shape[0]
    picked = jnp.take(operands, lists[1], axis=0)
    prods = jnp.einsum("bmi,bij->bmj", lmat, picked, preferred_element_type=jnp.float32)
    onehot = (lists[0][None, :] == jnp.arange(nblocks, dtype=jnp.int32)[:, None]).astype(
        jnp.float32
    )
    rows = jnp.einsum("rb,bmj->rmj", onehot, prods, precision=lax.Precision.HIGHEST)
    return rows.astype(jnp.bfloat16)


def exchange_blocks(xmat, listed):
    occ = xmat.shape[2] // 2
    left = jnp.take(xmat, listed[0], axis=0)
    right = jnp.take(xmat, listed[1], axis=0)
    swapped = jnp.concatenate([left[:, :, occ:], -left[:, :, :occ]], axis=2)
    kreal = jnp.einsum("emj,enj->emn", left, right, preferred_element_type=jnp.float32)
    kimag = jnp.einsum("emj,enj->emn", swapped, right, preferred_element_type=jnp.float32)
    return jnp.concatenate([kreal, kimag], axis=2)


def on_device(integrals, block_lists, coeff, match, ex_blocks):
    kdev = coeff.shape[0]
    nq = integrals.shape[0]
    adev = integrals.shape[2]
    edge = integrals.shape[4]
    occ = coeff.shape[3]
    nexch = ex_blocks.shape[2]
    naux = adev * lax.axis_size("fit")
    factor = -((nq * naux * occ) ** (-0.5))
    kglob = lax.axis_index("ka") * kdev + jnp.arange(kdev, dtype=jnp.int32)
    shards = lax.all_gather(coeff, "ka", axis=0, tiled=True)
    pending = jnp.zeros((kdev, nexch * edge, 2 * edge), jnp.float32)
    total = None
    for qq in range(nq):
        partner = jnp.take(match[qq], kglob, axis=0)
        partner_full = lax.all_gather(jnp.take(shards, partner, axis=0), "fit", axis=2, tiled=True)
        operands = block_operands(partner_full[0], edge)
        xmat = half_transform(integrals[qq, 0, 0], block_lists[qq, 0, 0], operands)
        summed = exchange_blocks(xmat, ex_blocks[0])
        blocks_all = [summed]
        flat = (jnp.stack(blocks_all) * factor).reshape(kdev, nexch * edge, 2 * edge)
        pending = pending + flat
    whole = lax.psum(pending, "fit")
    share = whole.shape[1] // lax.axis_size("fit")
    total = lax.dynamic_slice_in_dim(whole, lax.axis_index("fit") * share, share, 1)
    return total


def solution(mesh):
    return jax.shard_map(
        on_device,
        mesh=mesh,
        in_specs=(
            P(None, "ka", "fit", None, None, None),
            P(None, "ka", "fit", None, None),
            P("ka", None, "fit", None),
            P(),
            P("ka", None, None),
        ),
        out_specs=P("ka", "fit", None),
        check_vma=False,
    )
```

profile of v0, /device:TPU:94, one launch (start us, length us, event | category | flops | bytes accessed | tf_op | source)
XLA Modules:
  0.0 1852.3 jit_solution(7708082397937562943)
XLA Ops:
  14.4 9.4 all_gather.12
  28.2 346.1 %all-gather.6.cloned.1.call-done = bf16[1,2,1024,256]{3,2,1,0:T(8,128)(2,1)} async-done(((bf16[1,2,16,256]{3,2,1,0:T(8,128)(2,1)}), bf16[1,2,1024,256]{3,2,1,0:T(8,128)(2,1)}) %all-gather.6.cloned.1.call-update) | async-done | bytes 1048592 | tf_op jit(solution)/shard_map/all_gather | solution.py:52
  375.9 4.9 gather_fusion.3
  380.8 4.3 fusion.33
  385.1 5.7 fusion.47
  391.5 330.7 %all-gather.4.cloned.1.call-done = bf16[1,2,1024,256]{3,2,1,0:T(8,128)(2,1)} async-done(((bf16[1,2,16,256]{3,2,1,0:T(8,128)(2,1)}), bf16[1,2,1024,256]{3,2,1,0:T(8,128)(2,1)}) %all-gather.4.cloned.1.call-update) | async-done | bytes 1048592 | tf_op jit(solution)/shard_map/all_gather | solution.py:52
  723.8 5.4 gather_fusion
  729.1 4.3 fusion.30
  733.5 5.7 fusion.44
  739.8 2.8 gather_fusion.4
  742.6 2.8 gather_fusion.1
  745.4 2.9 gather_fusion.2
  748.3 2.9 gather_fusion.5
  751.2 318.9 %all-gather.8.cloned.1.call-done = bf16[1,2,1024,256]{3,2,1,0:T(8,128)(2,1)} async-done(((bf16[1,2,16,256]{3,2,1,0:T(8,128)(2,1)}), bf16[1,2,1024,256]{3,2,1,0:T(8,128)(2,1)}) %all-gather.8.cloned.1.call-update) | async-done | bytes 1048592 | tf_op jit(solution)/shard_map/all_gather | solution.py:52
  1071.7 5.1 gather_fusion.6
  1076.8 4.3 fusion.36
  1081.1 5.7 fusion.50
  1087.4 2.9 gather_fusion.7
  1090.3 2.8 gather_fusion.8
  1093.1 5.5 broadcast_select_fusion.3
  1098.6 2.3 fusion.82
  1101.1 1.9 copy-done.1
  1103.0 1.3 fusion.41
  1105.2 1.3 fusion.42
  1106.6 2.4 fusion.80
  1110.2 1.3 fusion.43
  1111.6 3.1 fusion.15
  1114.7 1.6 fusion.19
  1116.4 3.1 fusion.23
  1119.5 3.0 fusion.40
  1122.6 721.6 %all-reduce.2.cloned.1.call-done = f32[1,4096,128]{2,1,0:T(8,128)} async-done(((f32[1,4096,128]{2,1,0:T(8,128)}), f32[1,4096,128]{2,1,0:T(8,128)}) %all-reduce.2.cloned.1.call-update) | async-done | bytes 2097168 | tf_op jit(solution)/shard_map/psum | solution.py:59
  1844.1 1.4 constant_dynamic-slice_fusion.3
  (36 shorter events, 15.2 us)
Async XLA Ops:
  6.5 367.8 %all-gather.6.cloned.1.call-start = ((), (), s32[]{:S(2)}) async-start(), calls=%async_computation.1 | async-start | bytes 1064960 | tf_op jit(solution)/shard_map/all_gather | solution.py:52
  24.4 697.8 %all-gather.4.cloned.1.call-start = ((), (), s32[]{:S(2)}) async-start(), calls=%async_computation | async-start | bytes 1064960 | tf_op jit(solution)/shard_map/all_gather | solution.py:52
  25.1 1045.0 %all-gather.8.cloned.1.call-start = ((), (), s32[]{:S(2)}) async-start(), calls=%async_computation.2 | async-start | bytes 1064960 | tf_op jit(solution)/shard_map/all_gather | solution.py:52
  25.9 1818.3 %all-reduce.2.cloned.1.call-start = ((), (), s32[]{:S(2)}) async-start(), calls=%async_computation.3 | async-start | bytes 4194304 | tf_op jit(solution)/shard_map/psum | solution.py:59
  1100.8 2.2 copy-start.1
  1103.0 2.2 copy-start
  1106.5 3.7 copy-start.2
Sparse Core Ops, SparseCore 0:
  24.5 349.7 all-gather.5
  376.1 346.0 all-gather.3
  724.0 346.0 all-gather.7
  1122.7 721.4 all-reduce.1
where the time goes:
time: 1860 us; the launch traced here: 1850 us
  waiting for transfers between devices  1720 us (92%)
  local copies, waits for them, and re-layouts  44.9 us (2%)
  matrix products  42.1 us (2%)
  between operations  19.3 us (1%)
    all_gather x3, waiting for transfers between devices, on_device(): lax.all_gather(jnp.take(shards, partner, axis=0), 'fit', axis=2, tiled=True)  996 us
    psum x1, waiting for transfers between devices, on_device(): whole = lax.psum(pending, 'fit')  722 us
  transfers between devices with their start and end apart: 4, of which 4 were waited for; matrix products, arithmetic and copies ran while one was open for 3% of the time, Pallas kernels for 0%

commit v1 on v0

--- a/solution.py
+++ b/solution.py
@@ -2,6 +2,13 @@
 import jax.numpy as jnp
 from jax import lax
 from jax.sharding import PartitionSpec as P
+
+
+def return_all_the_target(in_array):
+    a_now = tuple((in_array for _ in range(lax.psum(1, "fit"))))
+    reply = jnp.stack(a_now, axis=0)
+    piece_now = lax.all_to_all(reply, axis_name="fit", split_axis=0, concat_axis=0)
+    return jnp.concatenate(piece_now, 2)
 
 
 def block_operands(coeff_one, edge):
@@ -49,7 +56,7 @@
     total = None
     for qq in range(nq):
         partner = jnp.take(match[qq], kglob, axis=0)
-        partner_full = lax.all_gather(jnp.take(shards, partner, axis=0), "fit", axis=2, tiled=True)
+        partner_full = return_all_the_target(jnp.take(shards, partner, axis=0))
         operands = block_operands(partner_full[0], edge)
         xmat = half_transform(integrals[qq, 0, 0], block_lists[qq, 0, 0], operands)
         summed = exchange_blocks(xmat, ex_blocks[0])

time: 1860 us -> 933 us (0.50)
  waiting for transfers between devices: 1720 us -> 741 us
  blocking collectives: 9.37 us -> 44.3 us
  starting transfers between devices: 0.12 us -> 22.3 us
    all_gather x3 -> x0, waiting for transfers between devices: 996 us -> none  [on_device(): lax.all_gather(jnp.take(shards, partner, axis=0), 'fit', axis=2, tiled=True)]
    all_to_all x0 -> x1, blocking collectives: none -> 35 us  [return_all_the_target(): lax.all_to_all(reply, axis_name='fit', split_axis=0, concat_axis=0)]
    all_to_all x0 -> x2, starting transfers between devices: none -> 21.9 us  [return_all_the_target(): lax.all_to_all(reply, axis_name='fit', split_axis=0, concat_axis=0)]
  transfers between devices with their start and end apart: 4 -> 3, of which waited for: 4 -> 2; matrix products, arithmetic and copies ran while one was open for 3% -> 5% of each run, Pallas kernels for 0% -> 0%
where the time goes in v1:
time: 933 us; the launch traced here: 929 us
  waiting for transfers between devices  741 us (79%)
  blocking collectives  44.3 us (5%)
  local copies, waits for them, and re-layouts  44 us (5%)
  matrix products  42.1 us (5%)
  starting transfers between devices  22.3 us (2%)
  between operations  19.4 us (2%)
  other arithmetic  15.6 us (2%)
    psum x1, waiting for transfers between devices, on_device(): whole = lax.psum(pending, 'fit')  723 us
    all_to_all x1, blocking collectives, return_all_the_target(): lax.all_to_all(reply, axis_name='fit', split_axis=0, concat_axis=0)  35 us
    all_to_all x2, starting transfers between devices, return_all_the_target(): lax.all_to_all(reply, axis_name='fit', split_axis=0, concat_axis=0)  21.9 us
  transfers between devices with their start and end apart: 3, of which 2 were waited for; matrix products, arithmetic and copies ran while one was open for 5% of the time, Pallas kernels for 0%

profile of v1, /device:TPU:94, one launch (start us, length us, event | category | flops | bytes accessed | tf_op | source)
XLA Modules:
  0.0 928.6 jit_solution(14827733496726697841)
XLA Ops:
  14.0 9.4 %all_gather.3 = bf16[4,2,16,256]{3,2,1,0:T(8,128)(2,1)S(1)} all-gather(bf16[1,2,16,256]{3,2,1,0:T(8,128)(2,1)} %param.13), channel_id=1, replica_groups=mesh['ka'=4,'fit'=64] {'ka'}, dimensions={0}, use_global_device_ids=true | all-gather | bytes 81920 | tf_op jit(solution)/shard_map/all_gather | solution.py:54
  23.5 35.0 %all_to_all.15 = bf16[64,1,2,16,256]{4,3,2,1,0:T(8,128)(2,1)S(1)} all-to-all(bf16[64,1,2,16,256]{4,3,2,1,0:T(8,128)(2,1)S(1)} %stack.7), channel_id=1, replica_groups=mesh['ka'=4,'fit'=64] {'fit'}, dimensions={0} | all-to-all | bytes 2097152 | tf_op jit(solution)/shard_map/all_to_all | solution.py:10
  59.6 10.6 %all-to-all-start.2 = ((bf16[64,1,2,16,256]{4,3,2,1,0:T(8,128)(2,1)}), bf16[64,1,2,16,256]{4,3,2,1,0:T(8,128)(2,1)S(1)}, u32[]{:S(2)}, u32[]{:S(2)}) async-start(bf16[64,1,2,16,256]{4,3,2,1,0:T(8,128)(2,1)} %stack.8), calls=%async_computation.2 | async-start | bytes 2097152 | tf_op jit(solution)/shard_map/all_to_all | solution.py:10
  70.7 5.0 gather_fusion.3
  75.6 17.6 %all-to-all-done.2 = bf16[64,1,2,16,256]{4,3,2,1,0:T(8,128)(2,1)S(1)} async-done(((bf16[64,1,2,16,256]{4,3,2,1,0:T(8,128)(2,1)}), bf16[64,1,2,16,256]{4,3,2,1,0:T(8,128)(2,1)S(1)}, u32[]{:S(2)}, u32[]{:S(2)}) %all-to-all-start.2) | async-done | bytes 1048608 | tf_op jit(solution)/shard_map/all_to_all | solution.py:10
  94.3 11.4 %all-to-all-start = ((bf16[64,1,2,16,256]{4,3,2,1,0:T(8,128)(2,1)}), bf16[64,1,2,16,256]{4,3,2,1,0:T(8,128)(2,1)}, u32[]{:S(2)}, u32[]{:S(2)}) async-start(bf16[64,1,2,16,256]{4,3,2,1,0:T(8,128)(2,1)} %stack.6), calls=%async_computation | async-start | bytes 2097152 | tf_op jit(solution)/shard_map/all_to_all | solution.py:10
  106.1 4.3 fusion.33
  110.4 5.7 fusion.47
  117.1 5.5 gather_fusion.6
  122.6 4.3 fusion.36
  126.9 5.7 fusion.50
  133.2 2.8 gather_fusion.4
  136.0 2.8 gather_fusion.7
  138.8 2.8 gather_fusion.8
  141.6 2.8 gather_fusion.5
  145.9 5.1 gather_fusion
  151.1 4.3 fusion.30
  155.4 5.7 fusion.44
  161.7 2.8 gather_fusion.1
  164.5 2.8 gather_fusion.2
  167.3 5.5 broadcast_select_fusion.3
  172.8 2.3 fusion.80
  175.4 1.9 copy-done.1
  177.3 1.3 fusion.43
  179.5 1.3 fusion.42
  180.8 2.4 fusion.82
  185.8 3.1 fusion.23
  189.0 1.6 fusion.19
  190.6 3.1 fusion.15
  193.8 3.0 fusion.40
  196.8 723.3 %all-reduce.2.cloned.1.call-done = f32[1,4096,128]{2,1,0:T(8,128)} async-done(((f32[1,4096,128]{2,1,0:T(8,128)}), f32[1,4096,128]{2,1,0:T(8,128)}) %all-reduce.2.cloned.1.call-update) | async-done | bytes 2097168 | tf_op jit(solution)/shard_map/psum | solution.py:66
  920.1 1.4 constant_dynamic-slice_fusion.3
  (39 shorter events, 12.5 us)
Async XLA Ops:
  6.5 63.7 %copy-start.3 = (s32[3,1,1,2,48]{4,3,2,1,0:T(2,128)S(1)}, s32[3,1,1,2,48]{4,3,2,1,0:T(2,128)}, u32[]{:S(2)}) copy-start(s32[3,1,1,2,48]{4,3,2,1,0:T(2,128)} %param.12) | copy-start | bytes 3460
  6.5 63.7 %copy-start.4 = (s32[1,2,64]{2,1,0:T(2,128)S(1)}, s32[1,2,64]{2,1,0:T(2,128)}, u32[]{:S(2)}) copy-start(s32[1,2,64]{2,1,0:T(2,128)} %param.15) | copy-start | bytes 1540
  59.6 33.6 %all-to-all-start.2 = ((bf16[64,1,2,16,256]{4,3,2,1,0:T(8,128)(2,1)}), bf16[64,1,2,16,256]{4,3,2,1,0:T(8,128)(2,1)S(1)}, u32[]{:S(2)}, u32[]{:S(2)}) async-start(bf16[64,1,2,16,256]{4,3,2,1,0:T(8,128)(2,1)} %stack.8), calls=%async_computation.2 | async-start | bytes 2097152 | tf_op jit(solution)/shard_map/all_to_all | solution.py:10
  94.3 50.0 %all-to-all-start = ((bf16[64,1,2,16,256]{4,3,2,1,0:T(8,128)(2,1)}), bf16[64,1,2,16,256]{4,3,2,1,0:T(8,128)(2,1)}, u32[]{:S(2)}, u32[]{:S(2)}) async-start(bf16[64,1,2,16,256]{4,3,2,1,0:T(8,128)(2,1)} %stack.6), calls=%async_computation | async-start | bytes 2097152 | tf_op jit(solution)/shard_map/all_to_all | solution.py:10
  105.7 814.4 %all-reduce.2.cloned.1.call-start = ((), (), s32[]{:S(2)}) async-start(), calls=%async_computation.3 | async-start | bytes 4194304 | tf_op jit(solution)/shard_map/psum | solution.py:66
  175.1 2.2 copy-start.1
  177.3 2.2 copy-start
  180.8 3.7 copy-start.2
Sparse Core Ops, SparseCore 0:
  196.9 723.1 all-reduce.1
